TPU v7x, 32 devices: a whole 2x2x4 slice. The times are simulated.
32 devices in a mesh: row: 4 (over y, core), col: 8 (over z, x).
Axes of the slice: x: 2, y: 2, z: 4, core: 2. Of those that a mesh axis runs over, the one named last changes fastest.
Arguments:
- layer_input: bfloat16 [256, 8192], P('row', 'col'), may hold values from -36 to 36, as said below
- norm_gain: float32 [8192], P('col'), may hold values from 0.1 to 1.9
- w_gate: bfloat16 [8192, 14336], P('col', 'row'), may hold values from -0.09375 to 0.09375
- w_up: bfloat16 [8192, 14336], P('col', 'row'), may hold values from -0.09375 to 0.09375
- w_down: bfloat16 [14336, 8192], P('row', 'col'), may hold values from -0.09375 to 0.09375
- mask_gate: int32 [64, 112], P('col', 'row'), may hold values 0 or 1
- mask_up: int32 [64, 112], P('col', 'row'), may hold values 0 or 1
- mask_down: int32 [112, 64], P('row', 'col'), may hold values 0 or 1
- out_grad: bfloat16 [256, 8192], P('row', 'col'), may hold values from -6 to 6
Outputs:
- layer_out: bfloat16 [256, 8192], P('row', 'col')
- input_grad: bfloat16 [256, 8192], P('row', 'col')
- gain_grad: float32 [8192], P('col')
- gate_wgrad: bfloat16 [8192, 14336], P('col', 'row')
- up_wgrad: bfloat16 [8192, 14336], P('col', 'row')
- down_wgrad: bfloat16 [14336, 8192], P('row', 'col')
Inputs may be any that keep to these rules, and one draw needn't show every extreme that they name: `layer_input`: the layer input's rows and features have scales that differ by up to a factor of ten.
All inputs are finite; a program needn't handle non-finite values. No bound on the sum of `mask_gate` or of `mask_up` or of `mask_down` on one device may be relied on, other than what follows from the above.
Results may differ from a plain program's by a relative error of at most 0.02.
Values may be sent and summed in bfloat16 or wider, within the bound.
A program may use at most 192 MiB of HBM per device.

v0:
```python
import jax
import jax.numpy as jnp
from jax import lax
from jax.sharding import PartitionSpec as P

D = 8192


norm_eps = 1e-05


def apply_mask(weight, mask):
    block_rows, block_cols = mask.shape
    row_count, col_count = weight.shape
    blocks = weight.reshape(
        block_rows, row_count // block_rows, block_cols, col_count // block_cols
    )
    keep = mask.astype(weight.dtype)[:, None, :, None]
    return (blocks * keep).reshape(row_count, col_count)


def contract_rows(left, right):
    return lax.dot_general(
        left, right, (((0,), (0,)), ((), ())), preferred_element_type=jnp.float32
    )


def contract_cols(left, right):
    return lax.dot_general(
        left, right, (((1,), (1,)), ((), ())), preferred_element_type=jnp.float32
    )


def shards(layer_input, norm_gain, w_gate, w_up, w_down, mask_gate, mask_up, mask_down, out_grad):
    x_float = layer_input.astype(jnp.float32)
    squares = jnp.sum(x_float * x_float, axis=1)
    totals = lax.psum(squares, "col")
    scale = lax.rsqrt(totals / D + norm_eps)[:, None]
    normed = (x_float * scale * norm_gain[None, :]).astype(jnp.bfloat16)
    eff_gate = apply_mask(w_gate, mask_gate)
    eff_up = apply_mask(w_up, mask_up)
    eff_down = apply_mask(w_down, mask_down)
    normed_all = lax.all_gather(normed, "row", axis=0, tiled=True)
    gate_part = jnp.dot(normed_all, eff_gate, preferred_element_type=jnp.float32)
    up_part = jnp.dot(normed_all, eff_up, preferred_element_type=jnp.float32)
    gate_mine, up_mine = (
        lax.psum_scatter(gate_part, "col", scatter_dimension=0, tiled=True),
        lax.psum_scatter(up_part, "col", scatter_dimension=0, tiled=True),
    )
    act_mine = (jax.nn.silu(gate_mine) * up_mine).astype(jnp.bfloat16)
    act_all = lax.all_gather(act_mine, "col", axis=0, tiled=True)
    down_part = jnp.dot(act_all, eff_down, preferred_element_type=jnp.float32)
    down_sum = lax.psum_scatter(
        down_part.astype(jnp.bfloat16), "row", scatter_dimension=0, tiled=True
    ).astype(jnp.float32)
    layer_out = (x_float + down_sum).astype(jnp.bfloat16)
    grad_all = lax.all_gather(out_grad, "row", axis=0, tiled=True)
    act_grad = lax.psum_scatter(
        contract_cols(grad_all, eff_down).astype(jnp.bfloat16),
        "col",
        scatter_dimension=0,
        tiled=True,
    ).astype(jnp.float32)
    down_wgrad = apply_mask(contract_rows(act_all, grad_all), mask_down).astype(jnp.bfloat16)
    sig = jax.nn.sigmoid(gate_mine)
    gate_grad = (act_grad * up_mine * sig * (1.0 + gate_mine * (1.0 - sig))).astype(jnp.bfloat16)
    up_grad = (act_grad * gate_mine * sig).astype(jnp.bfloat16)
    gate_grad_all, up_grad_all = (
        lax.all_gather(gate_grad, "col", axis=0, tiled=True),
        lax.all_gather(up_grad, "col", axis=0, tiled=True),
    )
    gate_wgrad = apply_mask(contract_rows(normed_all, gate_grad_all), mask_gate).astype(
        jnp.bfloat16
    )
    up_wgrad = apply_mask(contract_rows(normed_all, up_grad_all), mask_up).astype(jnp.bfloat16)
    normed_grad = lax.psum_scatter(
        (contract_cols(gate_grad_all, eff_gate) + contract_cols(up_grad_all, eff_up)).astype(
            jnp.bfloat16
        ),
        "row",
        scatter_dimension=0,
        tiled=True,
    ).astype(jnp.float32)
    gain_part = jnp.sum(normed_grad * x_float * scale, axis=0)
    dot_part = jnp.sum(normed_grad * norm_gain[None, :] * x_float, axis=1)
    gain_grad = lax.psum(gain_part, "row")
    dots = lax.psum(dot_part, "col")[:, None]
    input_grad = (
        out_grad.astype(jnp.float32)
        + scale * norm_gain[None, :] * normed_grad
        - x_float * scale * scale * scale * dots / D
    ).astype(jnp.bfloat16)
    return (layer_out, input_grad, gain_grad, gate_wgrad, up_wgrad, down_wgrad)


def solution(mesh):
    placed = (
        P("row", "col"),
        P("col"),
        P("col", "row"),
        P("col", "row"),
        P("row", "col"),
        P("col", "row"),
        P("col", "row"),
        P("row", "col"),
        P("row", "col"),
    )
    return jax.shard_map(
        shards,
        mesh=mesh,
        in_specs=placed,
        out_specs=(
            P("row", "col"),
            P("row", "col"),
            P("col"),
            P("col", "row"),
            P("col", "row"),
            P("row", "col"),
        ),
        check_vma=False,
    )
```

profile of v0, /device:TPU:1, one launch (start us, length us, event | category | flops | bytes accessed | tf_op | source)
XLA Modules:
  0.0 474.5 jit_solution(8949057064124700252)
XLA Ops:
  8.1 8.9 %all_gather.17 = bf16[256,1024]{1,0:T(8,128)(2,1)S(1)} all-gather(bf16[64,1024]{1,0:T(8,128)(2,1)} %param.17), channel_id=1, replica_groups=mesh['row'=4,'col'=8] {'row'}, dimensions={0}, use_global_device_ids=true | all-gather | bytes 655360 | tf_op jit(solution)/shard_map/all_gather | solution.py:57
  18.0 3.0 copy-done.2
  21.0 3.6 fusion.1
  24.8 10.4 %copy.19 = bf16[1024,3584]{0,1:T(8,128)(2,1)} copy(bf16[1024,3584]{1,0:T(8,128)(2,1)} %param.11) | data formatting | bytes 14680064 | tf_op args[2]
  35.4 17.9 %psum.21 = f32[64]{0:T(128)S(1)} all-reduce(f32[64]{0:T(128)S(1)} %fusion.24), channel_id=1, replica_groups=mesh['row'=4,'col'=8] {'col'}, use_global_device_ids=true, to_apply=%region_1.0 | all-reduce | flops 64 | bytes 512 | tf_op jit(solution)/shard_map/psum | solution.py:37
  53.4 10.8 %all_gather.15 = bf16[256,1024]{1,0:T(8,128)(2,1)S(1)} all-gather(bf16[64,1024]{1,0:T(8,128)(2,1)S(1)} %fusion.17), channel_id=1, replica_groups=mesh['row'=4,'col'=8] {'row'}, dimensions={0}, use_global_device_ids=true | all-gather | bytes 655360 | tf_op jit(solution)/shard_map/all_gather | solution.py:43
  65.2 3.0 copy-done.3
  68.3 4.0 fusion.3
  72.5 10.4 %copy.21 = bf16[1024,3584]{0,1:T(8,128)(2,1)} copy(bf16[1024,3584]{1,0:T(8,128)(2,1)} %param.12) | data formatting | bytes 14680064 | tf_op args[3]
  83.9 3.7 copy-done.4
  88.7 4.0 fusion.5
  92.7 82.4 %reduce-scatter.6.cloned.1.call-done = f32[32,3584]{1,0:T(8,128)} async-done(((f32[256,3584]{1,0:T(8,128)}), f32[32,3584]{1,0:T(8,128)}) %reduce-scatter.6.cloned.1.call-update) | async-done | bytes 458768 | tf_op jit(solution)/shard_map/reduce_scatter | solution.py:47
  175.1 84.3 %reduce-scatter.8.cloned.1.call-done = f32[32,3584]{1,0:T(8,128)} async-done(((f32[256,3584]{1,0:T(8,128)}), f32[32,3584]{1,0:T(8,128)}) %reduce-scatter.8.cloned.1.call-update) | async-done | bytes 458768 | tf_op jit(solution)/shard_map/reduce_scatter | solution.py:48
  259.4 2.3 fusion.12
  263.2 6.2 %mul.199 = f32[8,128,28,128]{1,0,3,2:T(8,128)} broadcast(f32[8,28]{0,1:T(8,128)S(1)} %copy.26), dimensions={0,2} | broadcast | bytes 14680960 | tf_op jit(solution)/shard_map/mul | solution.py:19
  269.5 14.2 %copy.54 = f32[448,8,8,128]{3,1,2,0:T(8,128)} copy(f32[448,8,8,128]{3,2,1,0:T(8,128)} %bitcast.64) | data formatting | bytes 29360128
  283.7 14.3 %copy.27 = f32[1024,3584]{1,0:T(8,128)} copy(f32[1024,3584]{0,1:T(8,128)} %bitcast.62) | data formatting | bytes 29360128 | tf_op jit(solution)/shard_map/mul | solution.py:19
  298.1 6.2 %mul.196 = f32[8,128,28,128]{1,0,3,2:T(8,128)} broadcast(f32[8,28]{0,1:T(8,128)S(1)} %copy.24), dimensions={0,2} | broadcast | bytes 14680960 | tf_op jit(solution)/shard_map/mul | solution.py:19
  304.2 14.1 %copy.55 = f32[448,8,8,128]{3,1,2,0:T(8,128)} copy(f32[448,8,8,128]{3,2,1,0:T(8,128)} %bitcast.65) | data formatting | bytes 29360128
  318.3 14.3 %copy.25 = f32[1024,3584]{1,0:T(8,128)} copy(f32[1024,3584]{0,1:T(8,128)} %bitcast.63) | data formatting | bytes 29360128 | tf_op jit(solution)/shard_map/mul | solution.py:19
  332.7 8.0 %fusion.2 = f32[256,1024]{1,0:T(8,128)S(1)} fusion(bf16[256,3584]{1,0:T(8,128)(2,1)} %all-gather.6.cloned.1.call-done, bf16[1024,3584]{0,1:T(8,128)(2,1)} %copy.19, bf16[448,8,8,128]{3,2,1,0:T(8,128)(2,1)} %bitcast.70), kind=kOutput, calls=%fused_computation.11 | convolution fusion | flops 1882718208 | bytes 17563648 | tf_op jit(solution)/shard_map/dot_general | solution.py:29
  340.7 13.4 %all-gather.8.cloned.1.call-done = bf16[256,3584]{1,0:T(8,128)(2,1)} async-done(((bf16[32,3584]{1,0:T(8,128)(2,1)}), bf16[256,3584]{1,0:T(8,128)(2,1)}) %all-gather.8.cloned.1.call-update) | async-done | bytes 1835024 | tf_op jit(solution)/shard_map/all_gather | solution.py:70
  354.1 8.6 %fusion.8 = bf16[256,1024]{1,0:T(8,128)(2,1)} fusion(f32[256,1024]{1,0:T(8,128)S(1)} %fusion.2, bf16[256,3584]{1,0:T(8,128)(2,1)} %all-gather.8.cloned.1.call-done, bf16[1024,3584]{0,1:T(8,128)(2,1)} %copy.21, bf16[448,8,8,128]{3,2,1,0:T(8,128)(2,1)} %bitcast.72), kind=kOutput, calls=%fused_computation.17 | convolution fusion | flops 1883242496 | bytes 18087936 | tf_op jit(solution)/shard_map/dot_general | solution.py:29
  363.0 38.3 %all-gather.4.cloned.1.call-done = bf16[256,3584]{1,0:T(8,128)(2,1)} async-done(((bf16[32,3584]{1,0:T(8,128)(2,1)}), bf16[256,3584]{1,0:T(8,128)(2,1)}) %all-gather.4.cloned.1.call-update) | async-done | bytes 1835024 | tf_op jit(solution)/shard_map/all_gather | solution.py:51
  401.2 8.6 %fusion.9 = bf16[256,1024]{1,0:T(8,128)(2,1)} fusion(bf16[256,3584]{1,0:T(8,128)(2,1)} %all-gather.4.cloned.1.call-done, bf16[3584,1024]{1,0:T(8,128)(2,1)} %param.13, bf16[448,8,8,128]{3,2,1,0:T(8,128)(2,1)} %bitcast.68), kind=kOutput, calls=%fused_computation.18 | convolution fusion | flops 1882980352 | bytes 17039360 | tf_op jit(solution)/shard_map/dot_general | solution.py:52
  409.9 10.7 %multiply_convert_fusion = bf16[1024,3584]{1,0:T(8,128)(2,1)} fusion(f32[1024,3584]{1,0:T(8,128)} %copy.27, bf16[256,1024]{1,0:T(8,128)(2,1)S(1)} %all_gather.15, bf16[256,3584]{1,0:T(8,128)(2,1)S(1)} %copy-done.8), kind=kOutput, calls=%fused_computation.4 | convolution fusion | flops 1886388224 | bytes 24379392 | tf_op jit(solution)/shard_map/dot_general | solution.py:23
  420.6 10.5 %multiply_convert_fusion.1 = bf16[1024,3584]{1,0:T(8,128)(2,1)} fusion(f32[1024,3584]{1,0:T(8,128)} %copy.25, bf16[256,1024]{1,0:T(8,128)(2,1)S(1)} %all_gather.15, bf16[256,3584]{1,0:T(8,128)(2,1)S(1)} %copy-done.7), kind=kOutput, calls=%fused_computation.5 | convolution fusion | flops 1886388224 | bytes 24379392 | tf_op jit(solution)/shard_map/dot_general | solution.py:23
  432.5 5.1 %fusion = bf16[3584,1024]{1,0:T(8,128)(2,1)} fusion(f32[448,8,8,128]{3,2,1,0:T(8,128)S(1)} %bitcast.66, bf16[256,3584]{1,0:T(8,128)(2,1)S(1)} %copy-done.6, bf16[256,1024]{1,0:T(8,128)(2,1)S(1)} %all_gather.17), kind=kOutput, calls=%fused_computation.1 | convolution fusion | flops 1886388224 | bytes 24379392 | tf_op jit(solution)/shard_map/dot_general | solution.py:23
  437.6 1.1 fusion.28
  438.8 16.7 %psum.22 = f32[64]{0:T(128)S(1)} all-reduce(f32[64]{0:T(128)S(1)} %get-tuple-element.7), channel_id=1, replica_groups=mesh['row'=4,'col'=8] {'col'}, use_global_device_ids=true, to_apply=%region_8.9 | all-reduce | flops 64 | bytes 512 | tf_op jit(solution)/shard_map/psum | solution.py:87
  455.5 10.4 %psum.23 = f32[1024]{0:T(1024)} all-reduce(f32[1024]{0:T(1024)S(1)} %get-tuple-element.6), channel_id=1, replica_groups=mesh['row'=4,'col'=8] {'row'}, use_global_device_ids=true, to_apply=%region_10.11 | all-reduce | flops 1024 | bytes 8192 | tf_op jit(solution)/shard_map/psum | solution.py:86
  465.9 1.8 fusion.22
  (61 shorter events, 9.1 us)
Async XLA Ops:
  7.2 85.6 %reduce-scatter.12.cloned.1.call-start = ((), (), s32[]{:S(2)}) async-start(), calls=%async_computation.9 | async-start | bytes 2064384 | tf_op jit(solution)/shard_map/reduce_scatter | solution.py:58
  8.1 12.9 %copy-start.13 = (bf16[3584,1024]{1,0:T(8,128)(2,1)S(1)}, bf16[3584,1024]{1,0:T(8,128)(2,1)}, u32[]{:S(2)}) copy-start(bf16[3584,1024]{1,0:T(8,128)(2,1)} %param.13) | copy-start | bytes 22020100
  18.0 3.0 copy-start.2
  21.0 3.7 copy-start.11
  24.6 150.5 %reduce-scatter.6.cloned.1.call-start = ((), (), s32[]{:S(2)}) async-start(), calls=%async_computation.5 | async-start | bytes 4128768 | tf_op jit(solution)/shard_map/reduce_scatter | solution.py:47
  24.8 10.4 %copy-start.5 = (bf16[64,1024]{1,0:T(8,128)(2,1)S(1)}, bf16[64,1024]{1,0:T(8,128)(2,1)}, u32[]{:S(2)}) copy-start(bf16[64,1024]{1,0:T(8,128)(2,1)} %param.9) | copy-start | bytes 393220
  24.8 28.5 %copy-start.10 = (f32[1024]{0:T(1024)S(1)}, f32[1024]{0:T(1024)}, u32[]{:S(2)}) copy-start(f32[1024]{0:T(1024)} %param.10) | copy-start | bytes 12292
  53.3 15.0 %copy-start = (bf16[1024,3584]{0,1:T(8,128)(2,1)S(1)}, bf16[1024,3584]{0,1:T(8,128)(2,1)}, u32[]{:S(2)}) copy-start(bf16[1024,3584]{0,1:T(8,128)(2,1)} %copy.19) | copy-start | bytes 22020100
  65.2 3.1 copy-start.3
  68.3 4.1 copy-start.12
  72.3 187.1 %reduce-scatter.8.cloned.1.call-start = ((), (), s32[]{:S(2)}) async-start(), calls=%async_computation.6 | async-start | bytes 4128768 | tf_op jit(solution)/shard_map/reduce_scatter | solution.py:48
  82.9 5.8 %copy-start.1 = (bf16[1024,3584]{0,1:T(8,128)(2,1)S(1)}, bf16[1024,3584]{0,1:T(8,128)(2,1)}, u32[]{:S(2)}) copy-start(bf16[1024,3584]{0,1:T(8,128)(2,1)} %copy.21) | copy-start | bytes 22020100
  83.9 3.7 copy-start.4
  92.7 240.1 %all-gather.6.cloned.1.call-start = ((), (), s32[]{:S(2)}) async-start(), calls=%async_computation.10 | async-start | bytes 2064384 | tf_op jit(solution)/shard_map/all_gather | solution.py:69
  261.8 92.3 %all-gather.8.cloned.1.call-start = ((), (), s32[]{:S(2)}) async-start(), calls=%async_computation.11 | async-start | bytes 2064384 | tf_op jit(solution)/shard_map/all_gather | solution.py:70
  262.4 138.9 %all-gather.4.cloned.1.call-start = ((), (), s32[]{:S(2)}) async-start(), calls=%async_computation.7 | async-start | bytes 2064384 | tf_op jit(solution)/shard_map/all_gather | solution.py:51
  262.9 174.7 %reduce-scatter.14.cloned.1.call-start = ((), (), s32[]{:S(2)}) async-start(), calls=%async_computation.12 | async-start | bytes 655360 | tf_op jit(solution)/shard_map/reduce_scatter | solution.py:76
  362.7 47.2 %copy-start.8 = (bf16[256,3584]{1,0:T(8,128)(2,1)S(1)}, bf16[256,3584]{1,0:T(8,128)(2,1)}, u32[]{:S(2)}) copy-start(bf16[256,3584]{1,0:T(8,128)(2,1)} %all-gather.8.cloned.1.call-done) | copy-start | bytes 5505028
  362.7 103.2 %reduce-scatter.10.cloned.1.call-start = ((), (), s32[]{:S(2)}) async-start(), calls=%async_computation.8 | async-start | bytes 655360 | tf_op jit(solution)/shard_map/reduce_scatter | solution.py:53
  409.9 10.7 %copy-start.7 = (bf16[256,3584]{1,0:T(8,128)(2,1)S(1)}, bf16[256,3584]{1,0:T(8,128)(2,1)}, u32[]{:S(2)}) copy-start(bf16[256,3584]{1,0:T(8,128)(2,1)} %all-gather.6.cloned.1.call-done) | copy-start | bytes 5505028
  431.0 1.5 copy-start.6
  432.5 33.3 %copy-start.9 = (bf16[64,1024]{1,0:T(8,128)(2,1)S(1)}, bf16[64,1024]{1,0:T(8,128)(2,1)}, u32[]{:S(2)}) copy-start(bf16[64,1024]{1,0:T(8,128)(2,1)} %param.17) | copy-start | bytes 393220
Sparse Core Ops, SparseCore 0:
  24.7 65.8 reduce-scatter.11
  94.3 80.7 reduce-scatter.5
  178.7 80.6 reduce-scatter.7
  261.9 44.9 all-gather.5
  309.0 45.0 all-gather.7
  356.1 45.0 all-gather.3
  403.7 21.8 reduce-scatter.13
  428.1 21.6 reduce-scatter.9
where the time goes:
time: 476 us; the launch traced here: 475 us
  waiting for transfers between devices  219 us (46%)
  local copies, waits for them, and re-layouts  106 us (22%)
  blocking collectives  64.7 us (14%)
  matrix products  63 us (13%)
  between operations  14.3 us (3%)
  other arithmetic  6.32 us (1%)
    reduce_scatter x1, waiting for transfers between devices, shards(): lax.psum_scatter(up_part, 'col', scatter_dimension=0, tiled=True)  84.3 us
    reduce_scatter x1, waiting for transfers between devices, shards(): lax.psum_scatter(gate_part, 'col', scatter_dimension=0, tiled=True)  82.4 us
    unnamed x32, local copies, waits for them, and re-layouts  60.4 us
    mul x8, local copies, waits for them, and re-layouts, apply_mask(): return (blocks * keep).reshape(row_count, col_count)  45 us
    all_gather x1, waiting for transfers between devices, shards(): act_all = lax.all_gather(act_mine, 'col', axis=0, tiled=True)  38.3 us
    dot_general x3, matrix products, contract_rows(): lax.dot_general(left, right, (((0,), (0,)), ((), ())), preferred_element_...  26.2 us
    dot_general x3, matrix products, contract_cols(): lax.dot_general(left, right, (((1,), (1,)), ((), ())), preferred_element_...  20.2 us
    psum x1, blocking collectives, shards(): totals = lax.psum(squares, 'col')  17.9 us
  transfers between devices with their start and end apart: 8, of which 4 were waited for; matrix products, arithmetic and copies ran while one was open for 33% of the time, Pallas kernels for 0%

commit v1 on v0

v1 whole, which is shorter than its diff:
```python
import functools

import jax
import jax.numpy as jnp
from jax import lax
from jax.experimental import pallas as pl
from jax.experimental.pallas import tpu as pltpu
from jax.sharding import PartitionSpec as P

BLK = 128
LANES = 128
MESH = pl.DeviceIdType.MESH
F32 = jnp.float32
BF16 = jnp.bfloat16
norm_eps = 1e-05


def dot_nn(left, right):
    return lax.dot_general(left, right, (((1,), (0,)), ((), ())), preferred_element_type=F32)


def dot_nt(left, right):
    return lax.dot_general(left, right, (((1,), (1,)), ((), ())), preferred_element_type=F32)


def dot_tn(left, right):
    return lax.dot_general(left, right, (((0,), (0,)), ((), ())), preferred_element_type=F32)


def chunk_width(hidden):
    for width in (512, 256, 128):
        if hidden % width == 0:
            return width
    return hidden


def layer_kernel(
    R, NZ, NX, width, total_width,
    x_ref, gain_ref, og_ref, mg_ref, mu_ref, md_ref, wg_hbm, wu_hbm, wd_hbm,
    out_ref, ig_ref, gg_out, act_all, gg_all, ug_all, nm_out, og_out,
    wg, wu, wd, nm_all, og_all, sq_mine, sq_all, part_a, part_g, xr_a, xr_g,
    red_a, red_g, zr_a, zr_g, ag, acc_d, acc_n, fin_s, fin_r, gn_mine, gn_all,
    dt_mine, dt_all,
    w_sem, og_s, og_r, nm_s, nm_r, sq_s, sq_r, xa_s, xa_r, xg_s, xg_r,
    za_s, za_r, zg_s, zg_r, agz_s, agz_r, agx_s, agx_r, fin_ss, fin_rs,
    gn_s, gn_r, dt_s, dt_r, loc_s,
):
    C = NZ * NX
    row = lax.axis_index("row")
    col = lax.axis_index("col")
    mz = col // NX
    mx = lax.rem(col, NX)
    rows, feats = x_ref.shape
    hidden = wg.shape[1]
    n = hidden // width
    T = part_a.shape[3]
    per = width // BLK

    def rpeer(k):
        return lax.rem(row + k, R)

    def cpeer(k):
        return lax.rem(col + k, C)

    def xpeer(k):
        return lax.rem(mx + k, NX)

    def zpeer(k):
        return lax.rem(mz + k, NZ)

    def remote(src, dst, ssem, rsem, dev):
        return pltpu.make_async_remote_copy(
            src_ref=src, dst_ref=dst, send_sem=ssem, recv_sem=rsem,
            device_id=dev, device_id_type=MESH,
        )

    barrier = pltpu.get_barrier_semaphore()
    for k in range(1, R):
        pl.semaphore_signal(barrier, inc=1, device_id=(rpeer(k), col), device_id_type=MESH)
    for k in range(1, C):
        pl.semaphore_signal(barrier, inc=1, device_id=(row, cpeer(k)), device_id_type=MESH)
    loads = [
        pltpu.make_async_copy(src, dst, w_sem.at[i])
        for i, (src, dst) in enumerate(((wd_hbm, wd), (wg_hbm, wg), (wu_hbm, wu)))
    ]
    for load in loads:
        load.start()
    pl.semaphore_wait(barrier, R - 1 + C - 1)

    def og_copy(src, dev):
        return remote(og_ref, og_all.at[src], og_s.at[dev], og_r.at[src], (dev, col))

    for k in range(1, R):
        og_copy(row, rpeer(k)).start()
    own_og = pltpu.make_async_copy(og_ref, og_all.at[row], loc_s.at[0])
    own_og.start()

    x = x_ref[...].astype(F32)
    tok = lax.broadcasted_iota(jnp.int32, (rows, LANES), 0)
    lane = lax.broadcasted_iota(jnp.int32, (rows, LANES), 1)
    diag = tok == lane

    def to_lanes(column):
        return jnp.sum(jnp.where(diag, column, 0.0), axis=0, keepdims=True)

    def to_column(line):
        return jnp.sum(jnp.where(diag, line, 0.0), axis=1, keepdims=True)

    sq_mine[...] = to_lanes(jnp.sum(x * x, axis=1, keepdims=True))

    def sq_copy(src, dev):
        return remote(sq_mine, sq_all.at[src], sq_s.at[dev], sq_r.at[src], (row, dev))

    for k in range(1, C):
        sq_copy(col, cpeer(k)).start()

    loads[0].wait()
    own_og.wait()
    for k in range(1, R):
        og_copy(rpeer(k), rpeer(k)).wait_recv()

    def xa_copy(j, src, dev):
        return remote(
            part_a.at[j, dev], xr_a.at[j, src], xa_s.at[j, dev], xa_r.at[j, src],
            (row, mz * NX + dev),
        )

    def xg_copy(j, src, dev):
        return remote(
            part_g.at[j, dev], xr_g.at[j, src], xg_s.at[j, dev], xg_r.at[j, src],
            (row, mz * NX + dev),
        )

    def a_part(j, carry):
        base = pl.multiple_of(j * width, width)
        for r in range(per):
            at = pl.ds(pl.multiple_of(base + r * BLK, BLK), BLK)
            wd[at, :] = wd[at, :] * md_ref[j * per + r].astype(BF16)
        a = dot_nt(
            og_all[...].reshape(R * rows, feats), wd[pl.ds(base, width), :]
        ).astype(BF16)
        for z in range(NZ):
            for xx in range(NX):
                c = z * NX + xx
                part_a[j, xx, z] = a[c * T : (c + 1) * T]
        for k in range(1, NX):
            xa_copy(j, mx, xpeer(k)).start()
        return carry

    lax.fori_loop(0, n, a_part, 0)

    sq_all[col] = sq_mine[...]
    for k in range(1, C):
        sq_copy(cpeer(k), cpeer(k)).wait_recv()
    total = sq_all[0]
    for c in range(1, C):
        total = total + sq_all[c]
    scale = lax.rsqrt(to_column(total) / total_width + norm_eps)
    gain = gain_ref[...]
    nm_all[row] = (x * scale * gain).astype(BF16)

    def nm_copy(src, dev):
        return remote(
            nm_all.at[src], nm_all.at[src], nm_s.at[dev], nm_r.at[src], (dev, col)
        )

    for k in range(1, R):
        nm_copy(row, rpeer(k)).start()
    loads[1].wait()
    loads[2].wait()

    def mask_columns(j, carry):
        cols = pl.ds(pl.multiple_of(j * width, width), width)
        for r in range(feats // BLK):
            at = slice(r * BLK, (r + 1) * BLK)
            wg[at, cols] = wg[at, cols] * mg_ref[r, :, cols].astype(BF16)
            wu[at, cols] = wu[at, cols] * mu_ref[r, :, cols].astype(BF16)
        return carry

    lax.fori_loop(0, n, mask_columns, 0)
    for k in range(1, R):
        nm_copy(rpeer(k), rpeer(k)).wait_recv()

    def g_part(j, carry):
        cols = pl.ds(pl.multiple_of(j * width, width), width)
        nm = nm_all[...].reshape(R * rows, feats)
        for which, w in enumerate((wg, wu)):
            p = dot_nn(nm, w[:, cols]).astype(BF16)
            for z in range(NZ):
                for xx in range(NX):
                    c = z * NX + xx
                    part_g[j, xx, z, which] = p[c * T : (c + 1) * T]
        for k in range(1, NX):
            xg_copy(j, mx, xpeer(k)).start()
        return carry

    lax.fori_loop(0, n, g_part, 0)

    def za_copy(j, src, dev):
        return remote(
            red_a.at[j, dev], zr_a.at[j, src], za_s.at[j, dev], za_r.at[j, src],
            (row, dev * NX + mx),
        )

    def zg_copy(j, src, dev):
        return remote(
            red_g.at[j, dev], zr_g.at[j, src], zg_s.at[j, dev], zg_r.at[j, src],
            (row, dev * NX + mx),
        )

    def a_sum(j, carry):
        for k in range(1, NX):
            xa_copy(j, xpeer(k), xpeer(k)).wait_recv()
        s = part_a[j, mx].astype(F32)
        for k in range(1, NX):
            s = s + xr_a[j, xpeer(k)].astype(F32)
        red_a[j] = s.astype(BF16)
        for k in range(1, NZ):
            za_copy(j, mz, zpeer(k)).start()
        return carry

    lax.fori_loop(0, n, a_sum, 0)

    def agz_copy(j, src, dev):
        return remote(
            ag.at[j, mx, src], ag.at[j, mx, src], agz_s.at[j, dev], agz_r.at[j, src],
            (row, dev * NX + mx),
        )

    def agx_copy(j, src, dev):
        return remote(
            ag.at[j, src], ag.at[j, src], agx_s.at[j, dev], agx_r.at[j, src],
            (row, mz * NX + dev),
        )

    def g_sum(j):
        for k in range(1, NX):
            xg_copy(j, xpeer(k), xpeer(k)).wait_recv()
        for z in range(NZ):
            s = part_g[j, mx, z].astype(F32)
            for k in range(1, NX):
                s = s + xr_g[j, xpeer(k), z].astype(F32)
            red_g[j, z] = s.astype(BF16)
        for k in range(1, NZ):
            zg_copy(j, mz, zpeer(k)).start()

    def pointwise(j):
        for k in range(1, NZ):
            za_copy(j, zpeer(k), zpeer(k)).wait_recv()
            zg_copy(j, zpeer(k), zpeer(k)).wait_recv()
        da = red_a[j, mz].astype(F32)
        gate = red_g[j, mz, 0].astype(F32)
        up = red_g[j, mz, 1].astype(F32)
        for k in range(1, NZ):
            zp = zpeer(k)
            da = da + zr_a[j, zp].astype(F32)
            gate = gate + zr_g[j, zp, 0].astype(F32)
            up = up + zr_g[j, zp, 1].astype(F32)
        sig = jax.nn.sigmoid(gate)
        ag[j, mx, mz, 0] = (gate * sig * up).astype(BF16)
        ag[j, mx, mz, 1] = (da * up * sig * (1.0 + gate * (1.0 - sig))).astype(BF16)
        ag[j, mx, mz, 2] = (da * gate * sig).astype(BF16)
        for k in range(1, NZ):
            agz_copy(j, mz, zpeer(k)).start()

    def forward_x(j):
        for k in range(1, NZ):
            agz_copy(j, zpeer(k), zpeer(k)).wait_recv()
        for k in range(1, NX):
            agx_copy(j, mx, xpeer(k)).start()

    def exchange(s, carry):
        @pl.when(s < n)
        def _():
            g_sum(s)

        @pl.when(jnp.logical_and(s >= 1, s < n + 1))
        def _():
            pointwise(s - 1)

        @pl.when(s >= 2)
        def _():
            forward_x(s - 2)

        return carry

    lax.fori_loop(0, n + 2, exchange, 0)

    acc_d[...] = jnp.zeros_like(acc_d)
    acc_n[...] = jnp.zeros_like(acc_n)

    def products(j, carry):
        for k in range(1, NX):
            agx_copy(j, xpeer(k), xpeer(k)).wait_recv()
        cols = pl.ds(pl.multiple_of(j * width, width), width)

        def tokens(which):
            return jnp.concatenate(
                [ag[j, c % NX, c // NX, which] for c in range(C)], axis=0
            )

        act, gg, ug = tokens(0), tokens(1), tokens(2)
        act_all[:, cols] = act
        gg_all[:, cols] = gg
        ug_all[:, cols] = ug
        acc_d[...] += dot_nn(act, wd[cols, :])
        acc_n[...] += dot_nt(gg, wg[:, cols]) + dot_nt(ug, wu[:, cols])
        return carry

    lax.fori_loop(0, n, products, 0)

    for r in range(R):
        at = slice(r * rows, (r + 1) * rows)
        fin_s[r, 0] = acc_d[at, :].astype(BF16)
        fin_s[r, 1] = acc_n[at, :].astype(BF16)

    def fin_copy(src, dev):
        return remote(
            fin_s.at[dev], fin_r.at[src], fin_ss.at[dev], fin_rs.at[src], (dev, col)
        )

    for k in range(1, R):
        fin_copy(row, rpeer(k)).start()
    nm_out[...] = nm_all[...].reshape(R * rows, feats)
    og_out[...] = og_all[...].reshape(R * rows, feats)
    for k in range(1, R):
        fin_copy(rpeer(k), rpeer(k)).wait_recv()
    down = fin_s[row, 0].astype(F32)
    ngrad = fin_s[row, 1].astype(F32)
    for k in range(1, R):
        down = down + fin_r[rpeer(k), 0].astype(F32)
        ngrad = ngrad + fin_r[rpeer(k), 1].astype(F32)
    x = x_ref[...].astype(F32)
    dt_mine[...] = to_lanes(jnp.sum(ngrad * gain * x, axis=1, keepdims=True))
    gn_mine[...] = jnp.sum(ngrad * x * scale, axis=0, keepdims=True)

    def dt_copy(src, dev):
        return remote(dt_mine, dt_all.at[src], dt_s.at[dev], dt_r.at[src], (row, dev))

    def gn_copy(src, dev):
        return remote(gn_mine, gn_all.at[src], gn_s.at[dev], gn_r.at[src], (dev, col))

    for k in range(1, C):
        dt_copy(col, cpeer(k)).start()
    for k in range(1, R):
        gn_copy(row, rpeer(k)).start()
    dt_all[col] = dt_mine[...]
    gn_all[row] = gn_mine[...]
    out_ref[...] = (x + down).astype(BF16)
    for k in range(1, C):
        dt_copy(cpeer(k), cpeer(k)).wait_recv()
    dots = dt_all[0]
    for c in range(1, C):
        dots = dots + dt_all[c]
    dots = to_column(dots)
    ig_ref[...] = (
        og_ref[...].astype(F32)
        + scale * gain * ngrad
        - x * scale * scale * scale * dots / total_width
    ).astype(BF16)
    for k in range(1, R):
        gn_copy(rpeer(k), rpeer(k)).wait_recv()
    gain_sum = gn_all[0]
    for r in range(1, R):
        gain_sum = gain_sum + gn_all[r]
    gg_out[...] = gain_sum

    for k in range(1, R):
        og_copy(row, rpeer(k)).wait_send()
        nm_copy(row, rpeer(k)).wait_send()
        fin_copy(row, rpeer(k)).wait_send()
        gn_copy(row, rpeer(k)).wait_send()
    for k in range(1, C):
        sq_copy(col, cpeer(k)).wait_send()
        dt_copy(col, cpeer(k)).wait_send()

    def drain(j, carry):
        for k in range(1, NX):
            xa_copy(j, mx, xpeer(k)).wait_send()
            xg_copy(j, mx, xpeer(k)).wait_send()
            agx_copy(j, mx, xpeer(k)).wait_send()
        for k in range(1, NZ):
            za_copy(j, mz, zpeer(k)).wait_send()
            zg_copy(j, mz, zpeer(k)).wait_send()
            agz_copy(j, mz, zpeer(k)).wait_send()
        return carry

    lax.fori_loop(0, n, drain, 0)


def wgrad_kernel(per, nm_ref, og_ref, act_ref, gg_ref, ug_ref, mg_ref, mu_ref, md_ref,
                 gw_ref, uw_ref, dw_ref):
    feats = nm_ref.shape[1]
    for src, mask, dst in ((gg_ref, mg_ref, gw_ref), (ug_ref, mu_ref, uw_ref)):
        w = dot_tn(nm_ref[...], src[...])
        for r in range(feats // BLK):
            at = slice(r * BLK, (r + 1) * BLK)
            dst[at, :] = (w[at, :] * mask[r]).astype(BF16)
    w = dot_tn(act_ref[...], og_ref[...])
    for r in range(per):
        at = slice(r * BLK, (r + 1) * BLK)
        dw_ref[at, :] = (w[at, :] * md_ref[r]).astype(BF16)


def shards(R, C, layer_input, norm_gain, w_gate, w_up, w_down,
           mask_gate, mask_up, mask_down, out_grad):
    rows, feats = layer_input.shape
    hidden = w_gate.shape[1]
    tokens = rows * R
    T = tokens // C
    NX = 1
    while (2 * NX) * (2 * NX) <= C:
        NX *= 2
    NZ = C // NX
    width = chunk_width(hidden)
    n = hidden // width
    per = width // BLK
    wide_gate = jnp.repeat(mask_gate.astype(F32), BLK, axis=1)[:, None, :]
    wide_up = jnp.repeat(mask_up.astype(F32), BLK, axis=1)[:, None, :]
    wide_down = jnp.repeat(mask_down.astype(F32), BLK, axis=1)[:, None, :]
    vm = pl.BlockSpec(memory_space=pltpu.VMEM)
    hbm = pl.BlockSpec(memory_space=pl.ANY)
    dma = pltpu.SemaphoreType.DMA
    V = pltpu.VMEM
    out_shapes = (
        ((rows, feats), BF16), ((rows, feats), BF16), ((1, feats), F32),
        ((tokens, hidden), BF16), ((tokens, hidden), BF16), ((tokens, hidden), BF16),
        ((tokens, feats), BF16), ((tokens, feats), BF16),
    )
    scratch = [
        V((feats, hidden), BF16), V((feats, hidden), BF16), V((hidden, feats), BF16),
        V((R, rows, feats), BF16), V((R, rows, feats), BF16),
        V((1, LANES), F32), V((C, 1, LANES), F32),
        V((n, NX, NZ, T, width), BF16), V((n, NX, NZ, 2, T, width), BF16),
        V((n, NX, NZ, T, width), BF16), V((n, NX, NZ, 2, T, width), BF16),
        V((n, NZ, T, width), BF16), V((n, NZ, 2, T, width), BF16),
        V((n, NZ, T, width), BF16), V((n, NZ, 2, T, width), BF16),
        V((n, NX, NZ, 3, T, width), BF16),
        V((tokens, feats), F32), V((tokens, feats), F32),
        V((R, 2, rows, feats), BF16), V((R, 2, rows, feats), BF16),
        V((1, feats), F32), V((R, 1, feats), F32),
        V((1, LANES), F32), V((C, 1, LANES), F32),
        dma((3,)),
        dma((R,)), dma((R,)), dma((R,)), dma((R,)), dma((C,)), dma((C,)),
        dma((n, NX)), dma((n, NX)), dma((n, NX)), dma((n, NX)),
        dma((n, NZ)), dma((n, NZ)), dma((n, NZ)), dma((n, NZ)),
        dma((n, NZ)), dma((n, NZ)), dma((n, NX)), dma((n, NX)),
        dma((R,)), dma((R,)), dma((R,)), dma((R,)), dma((C,)), dma((C,)),
        dma((1,)),
    ]
    layer_out, input_grad, gain_grad, act, gg, ug, nm, og = pl.pallas_call(
        functools.partial(layer_kernel, R, NZ, NX, width, float(feats * C)),
        out_shape=tuple(jax.ShapeDtypeStruct(s, t) for s, t in out_shapes),
        in_specs=[vm] * 6 + [hbm] * 3,
        out_specs=tuple([vm] * 8),
        scratch_shapes=scratch,
        compiler_params=pltpu.CompilerParams(
            collective_id=0, has_side_effects=True, vmem_limit_bytes=67043328
        ),
    )(layer_input, norm_gain[None, :], out_grad, wide_gate, wide_up, wide_down,
      w_gate, w_up, w_down)

    whole = lambda j: (0, 0)
    gate_wgrad, up_wgrad, down_wgrad = pl.pallas_call(
        functools.partial(wgrad_kernel, per),
        grid=(n,),
        out_shape=(
            jax.ShapeDtypeStruct((feats, hidden), BF16),
            jax.ShapeDtypeStruct((feats, hidden), BF16),
            jax.ShapeDtypeStruct((hidden, feats), BF16),
        ),
        in_specs=[
            pl.BlockSpec((tokens, feats), whole),
            pl.BlockSpec((tokens, feats), whole),
            pl.BlockSpec((tokens, width), lambda j: (0, j)),
            pl.BlockSpec((tokens, width), lambda j: (0, j)),
            pl.BlockSpec((tokens, width), lambda j: (0, j)),
            pl.BlockSpec((feats // BLK, 1, width), lambda j: (0, 0, j)),
            pl.BlockSpec((feats // BLK, 1, width), lambda j: (0, 0, j)),
            pl.BlockSpec((per, 1, feats), lambda j: (j, 0, 0)),
        ],
        out_specs=(
            pl.BlockSpec((feats, width), lambda j: (0, j)),
            pl.BlockSpec((feats, width), lambda j: (0, j)),
            pl.BlockSpec((width, feats), lambda j: (j, 0)),
        ),
        compiler_params=pltpu.CompilerParams(vmem_limit_bytes=40 * 1024 * 1024),
    )(nm, og, act, gg, ug, wide_gate, wide_up, wide_down)
    return (layer_out, input_grad, gain_grad[0], gate_wgrad, up_wgrad, down_wgrad)


def solution(mesh):
    placed = (
        P("row", "col"),
        P("col"),
        P("col", "row"),
        P("col", "row"),
        P("row", "col"),
        P("col", "row"),
        P("col", "row"),
        P("row", "col"),
        P("row", "col"),
    )
    return jax.shard_map(
        functools.partial(shards, mesh.shape["row"], mesh.shape["col"]),
        mesh=mesh,
        in_specs=placed,
        out_specs=(
            P("row", "col"),
            P("row", "col"),
            P("col"),
            P("col", "row"),
            P("col", "row"),
            P("row", "col"),
        ),
        check_vma=False,
    )
```

time: 476 us -> 215 us (0.45)
  waiting for transfers between devices: 219 us -> 0 us
  Pallas kernels: 0 us -> 196 us
  local copies, waits for them, and re-layouts: 106 us -> 15.7 us
  blocking collectives: 64.7 us -> 0 us
  matrix products: 63 us -> 0 us
  between operations: 14.3 us -> 0.69 us
    pallas_call x0 -> x2, Pallas kernels: none -> 196 us  [the longest x1 186 us: shards(): pl.pallas_call(functools.partial(layer_kernel, R, NZ, NX, width, float(fe...]
    reduce_scatter x5 -> x0, waiting for transfers between devices: 167 us -> none  [the longest x1 84.3 us: shards(): lax.psum_scatter(up_part, 'col', scatter_dimension=0, tiled=True)]
    dot_general x9 -> x0, matrix products: 63 us -> none  [the longest x3 26.2 us: contract_rows(): lax.dot_general(left, right, (((0,), (0,)), ((), ())), preferred_element_...]
    all_gather x3 -> x0, waiting for transfers between devices: 51.6 us -> none  [the longest x1 38.3 us: shards(): act_all = lax.all_gather(act_mine, 'col', axis=0, tiled=True)]
    unnamed x32 -> x21, local copies, waits for them, and re-layouts: 60.4 us -> 13 us
    psum x3 -> x0, blocking collectives: 45 us -> none  [the longest x1 17.9 us: shards(): totals = lax.psum(squares, 'col')]
    mul x8 -> x0, local copies, waits for them, and re-layouts: 45 us -> none  [apply_mask(): return (blocks * keep).reshape(row_count, col_count)]
    all_gather x2 -> x0, blocking collectives: 19.6 us -> none  [the longest x1 10.8 us: shards(): normed_all = lax.all_gather(normed, 'row', axis=0, tiled=True)]
  transfers between devices with their start and end apart: 8 -> 0, of which waited for: 4 -> 0; matrix products, arithmetic and copies ran while one was open for 33% -> 0% of each run, Pallas kernels for 0% -> 0%
where the time goes in v1:
time: 215 us; the launch traced here: 214 us
  Pallas kernels  196 us (91%)
  local copies, waits for them, and re-layouts  15.7 us (7%)
    pallas_call x1, Pallas kernels, shards(): pl.pallas_call(functools.partial(layer_kernel, R, NZ, NX, width, float(fe...  186 us
    unnamed x21, local copies, waits for them, and re-layouts  13 us
    pallas_call x1, Pallas kernels, shards(): pl.pallas_call(functools.partial(wgrad_kernel, per), grid=(n,), out_shape...  9.76 us

profile of v1, /device:TPU:1, one launch (start us, length us, event | category | flops | bytes accessed | tf_op | source)
XLA Modules:
  0.0 214.3 jit_solution(13671527743106612302)
XLA Ops:
  0.6 0.7 convert_element_type.9
  1.3 0.7 convert_element_type.10
  2.0 0.7 convert_element_type.11
  2.7 0.1 copy.18
  2.8 0.1 copy.17
  2.9 0.1 copy.16
  3.0 0.1 broadcast_bitcast_fusion.1
  3.1 0.8 copy.19.mg_ref
  3.8 0.1 broadcast_bitcast_fusion
  3.9 0.8 copy.20.mu_ref
  4.7 0.7 broadcast_in_dim.15
  5.4 186.1 %shard_map.136 = (bf16[64,1024]{1,0:T(8,128)(2,1)}, bf16[64,1024]{1,0:T(8,128)(2,1)}, f32[1,1024]{1,0:T(1,128)}, bf16[256,3584]{1,0:T(8,128)(2,1)}, bf16[256,358...) custom-call(bf16[64,1024]{1,0:T(8,128)(2,1)} %x_ref.1, ...), custom_call_target="tpu_custom_call" | custom-call | tf_op jit(solution)/shard_map/pallas_call | solution.py:451
  191.5 0.0 copy-start.8
  191.5 0.0 copy-start
  191.5 1.5 copy-done
  193.0 0.0 copy-start.1
  193.0 1.5 copy-done.1
  194.5 0.0 copy-start.2
  194.5 1.5 copy-done.2
  196.0 0.0 copy-start.3
  196.0 0.9 copy-done.3
  196.9 0.0 copy-start.4
  196.9 0.9 copy-done.4
  197.8 0.9 copy-done.5
  198.7 0.0 copy-start.6
  198.7 1.0 copy-done.6
  199.7 1.0 copy-done.7
  200.8 9.8 %shard_map.137 = (bf16[1024,3584]{1,0:T(8,128)(2,1)}, bf16[1024,3584]{1,0:T(8,128)(2,1)}, bf16[3584,1024]{1,0:T(8,128)(2,1)}) custom-call(bf16[256,1024]{1,0:T(8,128)(2,1)S(1)} %copy-done.6, bf16[256,1024]{1,0:T(8,128)(2,1)S(1)} %copy-done.7, bf16[256,3584]{1,0:T(8,128)(2,1)S(1)} %copy-done, bf16[256,3584]{1,0:T(8,128)(2,1)S(1)} %copy-done.1, ...), custom_call_target="tpu_custom_call" | custom-call | tf_op jit(solution)/shard_map/pallas_call | solution.py:464
  210.5 1.6 copy.26
  212.1 1.6 copy.27
  213.7 0.0 copy-done.8
  213.7 0.6 copy.28
  (2 shorter events, 0.0 us)
Async XLA Ops:
  191.5 22.2 %copy-start.8 = (f32[1,1024]{1,0:T(1,128)S(1)}, f32[1,1024]{1,0:T(1,128)}, u32[]{:S(2)}) copy-start(f32[1,1024]{1,0:T(1,128)} %get-tuple-element.19) | copy-start | bytes 12292
  191.5 1.5 copy-start
  193.0 1.5 copy-start.1
  194.5 1.5 copy-start.2
  196.0 0.9 copy-start.3
  196.9 0.9 copy-start.4
  197.8 0.9 copy-start.5
  198.7 1.0 copy-start.6
  199.7 1.0 copy-start.7

commit v2 on v1

--- a/solution.py
+++ b/solution.py
@@ -39,10 +39,10 @@
     x_ref, gain_ref, og_ref, mg_ref, mu_ref, md_ref, wg_hbm, wu_hbm, wd_hbm,
     out_ref, ig_ref, gg_out, act_all, gg_all, ug_all, nm_out, og_out,
     wg, wu, wd, nm_all, og_all, sq_mine, sq_all, part_a, part_g, xr_a, xr_g,
-    red_a, red_g, zr_a, zr_g, ag, acc_d, acc_n, fin_s, fin_r, gn_mine, gn_all,
+    red_a, red_g, zr_a, zr_g, cz_a, cz_g, da_sum, gu_sum, ag, acc_d, acc_n, fin_s, fin_r, gn_mine, gn_all,
     dt_mine, dt_all,
     w_sem, og_s, og_r, nm_s, nm_r, sq_s, sq_r, xa_s, xa_r, xg_s, xg_r,
-    za_s, za_r, zg_s, zg_r, agz_s, agz_r, agx_s, agx_r, fin_ss, fin_rs,
+    za_s, za_r, zg_s, zg_r, ca_r, cg_r, agz_s, agz_r, agf_s, agx_s, agx_r, fin_ss, fin_rs,
     gn_s, gn_r, dt_s, dt_r, loc_s,
 ):
     C = NZ * NX
@@ -196,17 +196,68 @@
 
     lax.fori_loop(0, n, g_part, 0)
 
-    def za_copy(j, src, dev):
-        return remote(
-            red_a.at[j, dev], zr_a.at[j, src], za_s.at[j, dev], za_r.at[j, src],
-            (row, dev * NX + mx),
-        )
-
-    def zg_copy(j, src, dev):
-        return remote(
-            red_g.at[j, dev], zr_g.at[j, src], zg_s.at[j, dev], zg_r.at[j, src],
-            (row, dev * NX + mx),
-        )
+    def inside(z):
+        return jnp.logical_and(z >= 0, z < NZ)
+
+    def outside(z):
+        return jnp.logical_or(z < 0, z >= NZ)
+
+    kinds = ((red_a, zr_a, cz_a, za_s, za_r, ca_r), (red_g, zr_g, cz_g, zg_s, zg_r, cg_r))
+
+    def z_near(kind, j, t, src):
+        red, zr, _, ssem, rsem, _ = kind
+        return remote(
+            red.at[j, t], zr.at[j, src], ssem.at[j, t], rsem.at[j, src], (row, t * NX + mx)
+        )
+
+    def z_chain(kind, j, t, step):
+        red, _, cz, ssem, _, csem = kind
+        return remote(
+            red.at[j, t], cz.at[j, t], ssem.at[j, t], csem.at[j, t],
+            (row, (mz + step) * NX + mx),
+        )
+
+    def z_send(kind, j, t, dist, sign):
+        if dist <= 2:
+            z_near(kind, j, t, mz).start()
+        else:
+            z_chain(kind, j, t, sign).start()
+
+    def z_first(kind, j):
+        for dist in range(1, NZ):
+            for sign in (1, -1):
+                t = mz + sign * dist
+                ready = inside(t)
+                if dist > 1:
+                    ready = jnp.logical_and(ready, outside(mz - sign))
+
+                @pl.when(ready)
+                def _():
+                    z_send(kind, j, t, dist, sign)
+
+    def z_between(kind, j):
+        red, cz = kind[0], kind[2]
+        for sign in (1, -1):
+            for dist in range(2, NZ):
+                t = mz + sign * dist
+
+                @pl.when(jnp.logical_and(inside(t), inside(mz - sign)))
+                def _():
+                    z_chain(kind, j, t, -sign).wait_recv()
+                    red[j, t] = (red[j, t].astype(F32) + cz[j, t].astype(F32)).astype(BF16)
+                    z_send(kind, j, t, dist, sign)
+
+    def z_last(kind, j, total):
+        red, zr = kind[0], kind[1]
+        total[...] = red[j, mz].astype(F32)
+        for dist in (1, 2):
+            for sign in (1, -1):
+                src = mz + sign * dist
+
+                @pl.when(inside(src))
+                def _():
+                    z_near(kind, j, src, src).wait_recv()
+                    total[...] += zr[j, src].astype(F32)
 
     def a_sum(j, carry):
         for k in range(1, NX):
@@ -215,8 +266,7 @@
         for k in range(1, NX):
             s = s + xr_a[j, xpeer(k)].astype(F32)
         red_a[j] = s.astype(BF16)
-        for k in range(1, NZ):
-            za_copy(j, mz, zpeer(k)).start()
+        z_first(kinds[0], j)
         return carry
 
     lax.fori_loop(0, n, a_sum, 0)
@@ -224,6 +274,12 @@
     def agz_copy(j, src, dev):
         return remote(
             ag.at[j, mx, src], ag.at[j, mx, src], agz_s.at[j, dev], agz_r.at[j, src],
+            (row, dev * NX + mx),
+        )
+
+    def agf_copy(j, src, dev):
+        return remote(
+            ag.at[j, mx, src], ag.at[j, mx, src], agf_s.at[j, src], agz_r.at[j, src],
             (row, dev * NX + mx),
         )
 
@@ -241,50 +297,63 @@
             for k in range(1, NX):
                 s = s + xr_g[j, xpeer(k), z].astype(F32)
             red_g[j, z] = s.astype(BF16)
-        for k in range(1, NZ):
-            zg_copy(j, mz, zpeer(k)).start()
+        z_first(kinds[1], j)
+
+    def between(j):
+        for kind in kinds:
+            z_between(kind, j)
 
     def pointwise(j):
-        for k in range(1, NZ):
-            za_copy(j, zpeer(k), zpeer(k)).wait_recv()
-            zg_copy(j, zpeer(k), zpeer(k)).wait_recv()
-        da = red_a[j, mz].astype(F32)
-        gate = red_g[j, mz, 0].astype(F32)
-        up = red_g[j, mz, 1].astype(F32)
-        for k in range(1, NZ):
-            zp = zpeer(k)
-            da = da + zr_a[j, zp].astype(F32)
-            gate = gate + zr_g[j, zp, 0].astype(F32)
-            up = up + zr_g[j, zp, 1].astype(F32)
+        z_last(kinds[0], j, da_sum)
+        z_last(kinds[1], j, gu_sum)
+        da = da_sum[...]
+        gate = gu_sum[0]
+        up = gu_sum[1]
         sig = jax.nn.sigmoid(gate)
         ag[j, mx, mz, 0] = (gate * sig * up).astype(BF16)
         ag[j, mx, mz, 1] = (da * up * sig * (1.0 + gate * (1.0 - sig))).astype(BF16)
         ag[j, mx, mz, 2] = (da * gate * sig).astype(BF16)
-        for k in range(1, NZ):
-            agz_copy(j, mz, zpeer(k)).start()
+        for dist in (1, 2):
+            for sign in (1, -1):
+                t = mz + sign * dist
+
+                @pl.when(inside(t))
+                def _():
+                    agz_copy(j, mz, t).start()
+
+    def pass_on(j, dists):
+        for dist in dists:
+            for sign in (1, -1):
+                src = mz - sign * dist
+
+                @pl.when(inside(src))
+                def _():
+                    agz_copy(j, src, src).wait_recv()
+
+                if dist >= 2:
+
+                    @pl.when(jnp.logical_and(inside(src), inside(mz + sign)))
+                    def _():
+                        agf_copy(j, src, mz + sign).start()
 
     def forward_x(j):
-        for k in range(1, NZ):
-            agz_copy(j, zpeer(k), zpeer(k)).wait_recv()
+        pass_on(j, range(3, NZ))
         for k in range(1, NX):
             agx_copy(j, mx, xpeer(k)).start()
 
     def exchange(s, carry):
-        @pl.when(s < n)
-        def _():
-            g_sum(s)
-
-        @pl.when(jnp.logical_and(s >= 1, s < n + 1))
-        def _():
-            pointwise(s - 1)
-
-        @pl.when(s >= 2)
-        def _():
-            forward_x(s - 2)
+        stages = (
+            g_sum, between, pointwise, lambda j: pass_on(j, range(1, min(3, NZ))), forward_x,
+        )
+        for depth, stage in enumerate(stages):
+
+            @pl.when(jnp.logical_and(s >= depth, s < n + depth))
+            def _():
+                stage(s - depth)
 
         return carry
 
-    lax.fori_loop(0, n + 2, exchange, 0)
+    lax.fori_loop(0, n + 4, exchange, 0)
 
     acc_d[...] = jnp.zeros_like(acc_d)
     acc_n[...] = jnp.zeros_like(acc_n)
@@ -380,16 +449,36 @@
             xg_copy(j, mx, xpeer(k)).wait_send()
             agx_copy(j, mx, xpeer(k)).wait_send()
         for k in range(1, NZ):
-            za_copy(j, mz, zpeer(k)).wait_send()
-            zg_copy(j, mz, zpeer(k)).wait_send()
-            agz_copy(j, mz, zpeer(k)).wait_send()
+            for kind in kinds:
+                z_near(kind, j, zpeer(k), mz).wait_send()
+        for dist in range(1, NZ):
+            for sign in (1, -1):
+                t = mz + sign * dist
+                if dist <= 2:
+
+                    @pl.when(inside(t))
+                    def _():
+                        agz_copy(j, mz, t).wait_send()
+
+                if dist >= 2:
+
+                    @pl.when(jnp.logical_and(inside(t), inside(mz - sign)))
+                    def _():
+                        agf_copy(j, t, mz - sign).wait_send()
+
         return carry
 
     lax.fori_loop(0, n, drain, 0)
 
 
 def wgrad_kernel(per, nm_ref, og_ref, act_ref, gg_ref, ug_ref, mg_ref, mu_ref, md_ref,
-                 gw_ref, uw_ref, dw_ref):
+                 lo_ref, ig_ref, gn_ref, gw_ref, uw_ref, dw_ref, lo_out, ig_out, gn_out):
+    @pl.when(pl.program_id(0) == 0)
+    def _():
+        lo_out[...] = lo_ref[...]
+        ig_out[...] = ig_ref[...]
+        gn_out[...] = gn_ref[...]
+
     feats = nm_ref.shape[1]
     for src, mask, dst in ((gg_ref, mg_ref, gw_ref), (ug_ref, mu_ref, uw_ref)):
         w = dot_tn(nm_ref[...], src[...])
@@ -435,6 +524,8 @@
         V((n, NX, NZ, T, width), BF16), V((n, NX, NZ, 2, T, width), BF16),
         V((n, NZ, T, width), BF16), V((n, NZ, 2, T, width), BF16),
         V((n, NZ, T, width), BF16), V((n, NZ, 2, T, width), BF16),
+        V((n, NZ, T, width), BF16), V((n, NZ, 2, T, width), BF16),
+        V((T, width), F32), V((2, T, width), F32),
         V((n, NX, NZ, 3, T, width), BF16),
         V((tokens, feats), F32), V((tokens, feats), F32),
         V((R, 2, rows, feats), BF16), V((R, 2, rows, feats), BF16),
@@ -443,8 +534,8 @@
         dma((3,)),
         dma((R,)), dma((R,)), dma((R,)), dma((R,)), dma((C,)), dma((C,)),
         dma((n, NX)), dma((n, NX)), dma((n, NX)), dma((n, NX)),
-        dma((n, NZ)), dma((n, NZ)), dma((n, NZ)), dma((n, NZ)),
-        dma((n, NZ)), dma((n, NZ)), dma((n, NX)), dma((n, NX)),
+        dma((n, NZ)), dma((n, NZ)), dma((n, NZ)), dma((n, NZ)), dma((n, NZ)), dma((n, NZ)),
+        dma((n, NZ)), dma((n, NZ)), dma((n, NZ)), dma((n, NX)), dma((n, NX)),
         dma((R,)), dma((R,)), dma((R,)), dma((R,)), dma((C,)), dma((C,)),
         dma((1,)),
     ]
@@ -461,13 +552,16 @@
       w_gate, w_up, w_down)
 
     whole = lambda j: (0, 0)
-    gate_wgrad, up_wgrad, down_wgrad = pl.pallas_call(
+    gate_wgrad, up_wgrad, down_wgrad, layer_out, input_grad, gain_grad = pl.pallas_call(
         functools.partial(wgrad_kernel, per),
         grid=(n,),
         out_shape=(
             jax.ShapeDtypeStruct((feats, hidden), BF16),
             jax.ShapeDtypeStruct((feats, hidden), BF16),
             jax.ShapeDtypeStruct((hidden, feats), BF16),
+            jax.ShapeDtypeStruct((rows, feats), BF16),
+            jax.ShapeDtypeStruct((rows, feats), BF16),
+            jax.ShapeDtypeStruct((1, feats), F32),
         ),
         in_specs=[
             pl.BlockSpec((tokens, feats), whole),
@@ -478,14 +572,20 @@
             pl.BlockSpec((feats // BLK, 1, width), lambda j: (0, 0, j)),
             pl.BlockSpec((feats // BLK, 1, width), lambda j: (0, 0, j)),
             pl.BlockSpec((per, 1, feats), lambda j: (j, 0, 0)),
+            pl.BlockSpec((rows, feats), whole),
+            pl.BlockSpec((rows, feats), whole),
+            pl.BlockSpec((1, feats), whole),
         ],
         out_specs=(
             pl.BlockSpec((feats, width), lambda j: (0, j)),
             pl.BlockSpec((feats, width), lambda j: (0, j)),
             pl.BlockSpec((width, feats), lambda j: (j, 0)),
+            pl.BlockSpec((rows, feats), whole),
+            pl.BlockSpec((rows, feats), whole),
+            pl.BlockSpec((1, feats), whole),
         ),
-        compiler_params=pltpu.CompilerParams(vmem_limit_bytes=40 * 1024 * 1024),
-    )(nm, og, act, gg, ug, wide_gate, wide_up, wide_down)
+        compiler_params=pltpu.CompilerParams(vmem_limit_bytes=67043328),
+    )(nm, og, act, gg, ug, wide_gate, wide_up, wide_down, layer_out, input_grad, gain_grad)
     return (layer_out, input_grad, gain_grad[0], gate_wgrad, up_wgrad, down_wgrad)
 
 

time: 215 us -> 191 us (0.89)
  local copies, waits for them, and re-layouts: 15.7 us -> 2.7 us
  Pallas kernels: 196 us -> 185 us
    pallas_call x1, Pallas kernels: 186 us -> 172 us  [shards(): pl.pallas_call(functools.partial(layer_kernel, R, NZ, NX, width, float(fe...]
    unnamed x21 -> x0, local copies, waits for them, and re-layouts: 13 us -> none
    pallas_call x1, Pallas kernels: 9.76 us -> 12.6 us  [shards(): pl.pallas_call(functools.partial(wgrad_kernel, per), grid=(n,), out_shape...]
where the time goes in v2:
time: 191 us
  Pallas kernels  185 us (97%)
  local copies, waits for them, and re-layouts  2.7 us (1%)
  other arithmetic  2.07 us (1%)
    pallas_call x1, Pallas kernels, shards(): pl.pallas_call(functools.partial(layer_kernel, R, NZ, NX, width, float(fe...  172 us
    pallas_call x1, Pallas kernels, shards(): pl.pallas_call(functools.partial(wgrad_kernel, per), grid=(n,), out_shape...  12.6 us

profile of v2, /device:TPU:1, one launch (start us, length us, event | category | flops | bytes accessed | tf_op | source)
XLA Modules:
  0.0 190.5 jit_solution(9833396501397645897)
XLA Ops:
  0.6 0.7 convert_element_type.9
  1.3 0.7 convert_element_type.10
  2.0 0.7 convert_element_type.11
  2.7 0.1 copy.18
  2.8 0.1 copy.17
  2.9 0.1 copy.16
  3.0 0.1 broadcast_bitcast_fusion.1
  3.1 0.8 copy.19.mg_ref
  3.8 0.1 broadcast_bitcast_fusion
  3.9 0.8 copy.20.mu_ref
  4.7 0.7 broadcast_in_dim.15
  5.4 172.5 %shard_map.136 = (bf16[64,1024]{1,0:T(8,128)(2,1)}, bf16[64,1024]{1,0:T(8,128)(2,1)}, f32[1,1024]{1,0:T(1,128)}, bf16[256,3584]{1,0:T(8,128)(2,1)}, bf16[256,358...) custom-call(bf16[64,1024]{1,0:T(8,128)(2,1)} %x_ref.1, ...), custom_call_target="tpu_custom_call" | custom-call | tf_op jit(solution)/shard_map/pallas_call | solution.py:542
  177.9 12.6 %shard_map.137 = (bf16[1024,3584]{1,0:T(8,128)(2,1)}, bf16[1024,3584]{1,0:T(8,128)(2,1)}, bf16[3584,1024]{1,0:T(8,128)(2,1)}, bf16[64,1024]{1,0:T(8,128)(2,1)}, ...) custom-call(bf16[256,1024]{1,0:T(8,128)(2,1)} %get-tuple-element.20.nm_ref, bf16[256,1024]{1,0:T(8,128)(2,1)} %get-tuple-element.21.og_ref, ...), custom_call_target="tpu_custom_call" | custom-call | tf_op jit(solution)/shard_map/pallas_call | solution.py:555

commit v3 on v2

--- a/solution.py
+++ b/solution.py
@@ -27,8 +27,8 @@
     return lax.dot_general(left, right, (((0,), (0,)), ((), ())), preferred_element_type=F32)
 
 
-def chunk_width(hidden):
-    for width in (512, 256, 128):
+def chunk_width(hidden, widths):
+    for width in widths:
         if hidden % width == 0:
             return width
     return hidden
@@ -501,7 +501,7 @@
     while (2 * NX) * (2 * NX) <= C:
         NX *= 2
     NZ = C // NX
-    width = chunk_width(hidden)
+    width = chunk_width(hidden, (256, 128))
     n = hidden // width
     per = width // BLK
     wide_gate = jnp.repeat(mask_gate.astype(F32), BLK, axis=1)[:, None, :]
@@ -551,6 +551,9 @@
     )(layer_input, norm_gain[None, :], out_grad, wide_gate, wide_up, wide_down,
       w_gate, w_up, w_down)
 
+    width = chunk_width(hidden, (512, 256, 128))
+    n = hidden // width
+    per = width // BLK
     whole = lambda j: (0, 0)
     gate_wgrad, up_wgrad, down_wgrad, layer_out, input_grad, gain_grad = pl.pallas_call(
         functools.partial(wgrad_kernel, per),

time: 191 us -> 184 us (0.963)
  Pallas kernels: 185 us -> 179 us
    pallas_call x1, Pallas kernels: 172 us -> 166 us  [shards(): pl.pallas_call(functools.partial(layer_kernel, R, NZ, NX, width, float(fe...]
where the time goes in v3:
time: 184 us
  Pallas kernels  179 us (97%)
  local copies, waits for them, and re-layouts  2.7 us (1%)
  other arithmetic  2.07 us (1%)
    pallas_call x1, Pallas kernels, shards(): pl.pallas_call(functools.partial(layer_kernel, R, NZ, NX, width, float(fe...  166 us
    pallas_call x1, Pallas kernels, shards(): pl.pallas_call(functools.partial(wgrad_kernel, per), grid=(n,), out_shape...  12.6 us

profile of v3, /device:TPU:1, one launch (start us, length us, event | category | flops | bytes accessed | tf_op | source)
XLA Modules:
  0.0 184.0 jit_solution(1757267010478650300)
XLA Ops:
  0.6 0.7 convert_element_type.9
  1.3 0.7 convert_element_type.10
  2.0 0.7 convert_element_type.11
  2.7 0.1 copy.18
  2.8 0.1 copy.17
  2.9 0.1 copy.16
  3.0 0.1 broadcast_bitcast_fusion.1
  3.1 0.8 copy.19.mg_ref
  3.8 0.1 broadcast_bitcast_fusion
  3.9 0.8 copy.20.mu_ref
  4.7 0.7 broadcast_in_dim.15
  5.4 165.9 %shard_map.136 = (bf16[64,1024]{1,0:T(8,128)(2,1)}, bf16[64,1024]{1,0:T(8,128)(2,1)}, f32[1,1024]{1,0:T(1,128)}, bf16[256,3584]{1,0:T(8,128)(2,1)}, bf16[256,358...) custom-call(bf16[64,1024]{1,0:T(8,128)(2,1)} %x_ref.1, ...), custom_call_target="tpu_custom_call" | custom-call | tf_op jit(solution)/shard_map/pallas_call | solution.py:542
  171.4 12.6 %shard_map.137 = (bf16[1024,3584]{1,0:T(8,128)(2,1)}, bf16[1024,3584]{1,0:T(8,128)(2,1)}, bf16[3584,1024]{1,0:T(8,128)(2,1)}, bf16[64,1024]{1,0:T(8,128)(2,1)}, ...) custom-call(bf16[256,1024]{1,0:T(8,128)(2,1)} %get-tuple-element.20.nm_ref, bf16[256,1024]{1,0:T(8,128)(2,1)} %get-tuple-element.21.og_ref, ...), custom_call_target="tpu_custom_call" | custom-call | tf_op jit(solution)/shard_map/pallas_call | solution.py:558
